TPU v7x, 512 devices: a whole 4x4x16 slice. The times are simulated.
512 devices in a mesh: pair: 64 (over z, y), virt: 8 (over x, core).
Axes of the slice: x: 4, y: 4, z: 16, core: 2. Of those that a mesh axis runs over, the one named last changes fastest.
Arguments:
- amplitudes: bfloat16 [512, 8, 4096], P('pair', 'virt'), may hold values from -6 to 6
- partner: int32 [512], P('pair'), may hold values from 0 to 511, as said below
- integrals: bfloat16 [64, 4096, 4096], P('virt', 'pair'), may hold values from -0.09375 to 0.09375
- pattern: int32 [64], P('virt'), may hold values from 0 to 15, as said below
- owner: int32 [16], replicated, may hold values from 0 to 15, as said below
Outputs:
- ladder: bfloat16 [512, 16, 4096], P('pair', 'virt')
Inputs may be any that keep to these rules, and one draw needn't show every extreme that they name: partner pairs each pair with another one and is its own inverse; the partner of a pair held by index j of pair is held by index j + 64 / 2 modulo 64, that is half the pair axis away. `pattern`: every ab tile pair appears exactly four times in all. owner names every ab tile pair exactly once.
All inputs are finite; a program needn't handle non-finite values.
Results may differ from a plain program's by a relative error of at most 0.0051.
Values may be sent and summed in bfloat16 or wider, within the bound.
A program may use at most 64 MiB of HBM per device.

v0:
```python
import jax
import jax.numpy as jnp
from jax import lax
from jax.sharding import PartitionSpec as P

TILE = 64


def from_partner(value, axis, stride):
    mask = 2**stride
    pairs = [(source, source ^ mask) for source in range(lax.axis_size(axis))]
    return lax.ppermute(value, axis, pairs)


def symmetrize(plain, mirrored):
    count, width = (plain.shape[0], plain.shape[1])
    flipped = jnp.swapaxes(mirrored.reshape(count, width, TILE, TILE), 2, 3).reshape(plain.shape)
    return (plain.astype(jnp.float32) + flipped.astype(jnp.float32)).astype(jnp.bfloat16)


def shards(amplitudes, partner, integrals, pattern, owner):
    rows = amplitudes.shape[0]
    top_bit = lax.axis_size("pair").bit_length() - 2
    other = from_partner(amplitudes, "pair", top_bit)
    symmetric = symmetrize(amplitudes, jnp.take(other, partner % rows, axis=0))
    piece = lax.all_gather(symmetric, "pair", axis=0, tiled=True)
    flat = piece.reshape(piece.shape[0], -1)
    terms = jnp.einsum("rc,kjc->rkj", flat, integrals, preferred_element_type=jnp.float32)
    selector = (owner[None, :] == pattern[:, None]).astype(jnp.float32)
    spread = jnp.einsum("pkj,ks->psj", terms, selector, precision=lax.Precision.HIGHEST)
    routed = lax.all_to_all(spread, "pair", split_axis=0, concat_axis=2, tiled=True)
    summed = lax.psum_scatter(routed, "virt", scatter_dimension=1, tiled=True)
    result = summed.astype(jnp.bfloat16)
    return result


def solution(mesh):
    return jax.shard_map(
        shards,
        mesh=mesh,
        in_specs=(P("pair", "virt", None), P("pair"), P("virt", "pair", None), P("virt"), P()),
        out_specs=P("pair", "virt", None),
        check_vma=False,
    )
```

profile of v0, /device:TPU:8, one launch (start us, length us, event | category | flops | bytes accessed | tf_op | source)
XLA Modules:
  0.0 357.5 jit_solution(16470699635944835072)
XLA Ops:
  6.5 0.0 all-gather.2.cloned.1.call-start
  6.5 15.7 %collective-permute-start = (bf16[8,1,4096]{2,0,1:T(8,128)(2,1)}, bf16[8,1,4096]{2,0,1:T(8,128)(2,1)S(1)}, u32[]{:S(2)}, u32[]{:S(2)}) collective-permute-start(bf16[8,1,4096]{2,0,1:T(8,128)(2,1)} %param.5), channel_id=1, source_target_pairs={{0,256},{8,264},{16,272},{24,280},{32,288},{40,296},{48,304},{56,3... | collective-permute-start | bytes 196616 | tf_op jit(solution)/shard_map/ppermute | solution.py:12
  22.3 0.7 compare_and_fusion
  22.9 3.8 %collective-permute-done = bf16[8,1,4096]{2,0,1:T(8,128)(2,1)S(1)} collective-permute-done((bf16[8,1,4096]{2,0,1:T(8,128)(2,1)}, bf16[8,1,4096]{2,0,1:T(8,128)(2,1)S(1)}, u32[]{:S(2)}, u32[]{:S(2)}) %collective-permute-start) | collective-permute-done | bytes 65568 | tf_op jit(solution)/shard_map/ppermute | solution.py:12
  26.8 0.6 gather_fusion
  27.4 0.2 gather.7
  27.5 0.1 copy.21
  27.7 0.1 convert_bitcast_fusion
  27.8 0.1 reshape.45
  27.9 1.5 add_convert_fusion
  29.4 0.0 all-gather.2.cloned.1.call-update
  29.4 0.0 copy-start
  29.4 0.0 copy-start.1
  29.4 0.0 reduce-scatter.2.cloned.1.call-start
  29.5 146.3 %all-gather.2.cloned.1.call-done = bf16[512,1,4096]{2,0,1:T(8,128)(2,1)} async-done(((bf16[8,1,4096]{2,0,1:T(8,128)(2,1)}), bf16[512,1,4096]{2,0,1:T(8,128)(2,1)}) %all-gather.2.cloned.1.call-update) | async-done | bytes 4194320 | tf_op jit(solution)/shard_map/all_gather | solution.py:26
  175.8 6.3 %fusion = f32[512,8,64]{0,1,2:T(8,128)S(1)} fusion(bf16[512,1,4096]{2,0,1:T(8,128)(2,1)} %all-gather.2.cloned.1.call-done, bf16[8,64,4096]{2,1,0:T(8,128)(2,1)} %param.7), kind=kOutput, calls=%fused_computation.1 | convolution fusion | flops 2147483648 | bytes 9437184 | tf_op jit(solution)/shard_map/rc,kjc->rkj/dot_general | solution.py:28
  182.1 0.0 copy-done
  182.1 0.0 copy-done.1
  182.1 1.1 convolution_bitcast_fusion
  183.2 4.2 %copy.23 = f32[512,16,64]{2,1,0:T(8,128)} copy(f32[512,16,64]{0,1,2:T(8,128)S(1)} %convolution_bitcast_fusion) | data formatting | bytes 4194304 | tf_op jit(solution)/shard_map/pkj,ks->psj/transpose | solution.py:30
  187.4 4.6 %reshape.61 = f32[64,1,8192]{2,1,0:T(1,128)S(1)} reshape(f32[512,16,64]{2,1,0:T(8,128)} %copy.23) | data formatting | bytes 4194304
  192.0 101.3 %all_to_all.18 = f32[64,1,8192]{2,1,0:T(1,128)} all-to-all(f32[64,1,8192]{2,1,0:T(1,128)S(1)} %reshape.61), channel_id=1, replica_groups=mesh['pair'=64,'virt'=8] {'pair'}, dimensions={0} | all-to-all | bytes 4194304 | tf_op jit(solution)/shard_map/all_to_all | solution.py:31
  293.3 0.5 broadcast.45
  293.8 7.5 %reduce = f32[64,8192]{1,0:T(8,128)S(1)} reduce(f32[64,1,8192]{2,1,0:T(1,128)} %all_to_all.18, f32[]{:T(128)} %broadcast.45), dimensions={1}, to_apply=%all_to_all.13.reduce_sub_computation | reduce | bytes 4194308 | tf_op jit(solution)/shard_map/all_to_all | solution.py:31
  301.3 3.0 reshape.62
  304.4 6.6 %copy.27 = f32[8,16,64,64]{3,2,0,1:T(8,128)} copy(f32[8,16,64,64]{3,1,0,2:T(8,128)} %bitcast.24) | data formatting | bytes 4194304 | tf_op jit(solution)/shard_map/all_to_all | solution.py:31
  310.9 4.8 %reshape.60 = f32[8,16,4096]{2,0,1:T(8,128)} reshape(f32[8,16,64,64]{3,2,0,1:T(8,128)} %copy.27) | data formatting | bytes 4194304 | tf_op jit(solution)/shard_map/all_to_all | solution.py:31
  315.7 0.0 reduce-scatter.2.cloned.1.call-update
  315.7 33.2 %reduce-scatter.2.cloned.1.call-done = f32[8,2,4096]{2,0,1:T(8,128)} async-done(((f32[8,16,4096]{2,0,1:T(8,128)}), f32[8,2,4096]{2,0,1:T(8,128)}) %reduce-scatter.2.cloned.1.call-update) | async-done | bytes 262160 | tf_op jit(solution)/shard_map/reduce_scatter | solution.py:32
  348.9 1.0 convert_element_type.32
  349.9 0.8 copy.26
  (1 shorter events, 0.0 us)
Async XLA Ops:
  6.5 169.3 %all-gather.2.cloned.1.call-start = ((), (), s32[]{:S(2)}) async-start(), calls=%async_computation.2 | async-start | bytes 4259840 | tf_op jit(solution)/shard_map/all_gather | solution.py:26
  6.5 20.2 %collective-permute-start = (bf16[8,1,4096]{2,0,1:T(8,128)(2,1)}, bf16[8,1,4096]{2,0,1:T(8,128)(2,1)S(1)}, u32[]{:S(2)}, u32[]{:S(2)}) collective-permute-start(bf16[8,1,4096]{2,0,1:T(8,128)(2,1)} %param.5), channel_id=1, source_target_pairs={{0,256},{8,264},{16,272},{24,280},{32,288},{40,296},{48,304},{56,3... | collective-permute-start | bytes 196616 | tf_op jit(solution)/shard_map/ppermute | solution.py:12
  29.4 152.7 %copy-start = (s32[16]{0:T(128)S(1)}, s32[16]{0:T(128)}, u32[]{:S(2)}) copy-start(s32[16]{0:T(128)} %param.9) | copy-start | bytes 196
  29.4 152.7 %copy-start.1 = (s32[8]{0:T(128)S(1)}, s32[8]{0:T(128)}, u32[]{:S(2)}) copy-start(s32[8]{0:T(128)} %param.8) | copy-start | bytes 100
  29.4 319.5 %reduce-scatter.2.cloned.1.call-start = ((), (), s32[]{:S(2)}) async-start(), calls=%async_computation.3 | async-start | bytes 2359296 | tf_op jit(solution)/shard_map/reduce_scatter | solution.py:32
Sparse Core Ops, SparseCore 0:
  29.5 146.2 all-gather.1
  315.8 33.0 reduce-scatter.1
where the time goes:
time: 358 us
  waiting for transfers between devices  183 us (51%)
  blocking collectives  101 us (28%)
  local copies, waits for them, and re-layouts  25.4 us (7%)
  starting transfers between devices  15.8 us (4%)
  between operations  13.5 us (4%)
  other arithmetic  10.7 us (3%)
  matrix products  7.4 us (2%)
    all_gather x1, waiting for transfers between devices, shards(): piece = lax.all_gather(symmetric, 'pair', axis=0, tiled=True)  146 us
    all_to_all x1, blocking collectives, shards(): lax.all_to_all(spread, 'pair', split_axis=0, concat_axis=2, tiled=True)  101 us
    reduce_scatter x1, waiting for transfers between devices, shards(): summed = lax.psum_scatter(routed, 'virt', scatter_dimension=1, tiled=True)  33.2 us
    ppermute x1, starting transfers between devices, from_partner(): return lax.ppermute(value, axis, pairs)  15.7 us
    all_to_all x3, local copies, waits for them, and re-layouts, shards(): lax.all_to_all(spread, 'pair', split_axis=0, concat_axis=2, tiled=True)  11.8 us
    unnamed x6, local copies, waits for them, and re-layouts  7.61 us
    all_to_all x1, other arithmetic, shards(): lax.all_to_all(spread, 'pair', split_axis=0, concat_axis=2, tiled=True)  7.54 us
  transfers between devices with their start and end apart: 3, of which 3 were waited for; matrix products, arithmetic and copies ran while one was open for 0% of the time, Pallas kernels for 0%

commit v1 on v0

--- a/solution.py
+++ b/solution.py
@@ -23,7 +23,9 @@
     top_bit = lax.axis_size("pair").bit_length() - 2
     other = from_partner(amplitudes, "pair", top_bit)
     symmetric = symmetrize(amplitudes, jnp.take(other, partner % rows, axis=0))
-    piece = lax.all_gather(symmetric, "pair", axis=0, tiled=True)
+    piece = jnp.concatenate(
+        lax.all_to_all(jnp.stack([symmetric] * lax.axis_size("pair")), "pair", 0, 0), axis=0
+    )
     flat = piece.reshape(piece.shape[0], -1)
     terms = jnp.einsum("rc,kjc->rkj", flat, integrals, preferred_element_type=jnp.float32)
     selector = (owner[None, :] == pattern[:, None]).astype(jnp.float32)

time: 358 us -> 413 us (1.15)
  blocking collectives: 101 us -> 306 us
  waiting for transfers between devices: 183 us -> 37.1 us
    all_to_all x0 -> x1, blocking collectives: none -> 203 us  [shards(): lax.all_to_all(jnp.stack([symmetric] * lax.axis_size('pair')), 'pair', 0, 0)]
    all_gather x1 -> x0, waiting for transfers between devices: 146 us -> none  [shards(): piece = lax.all_gather(symmetric, 'pair', axis=0, tiled=True)]
  transfers between devices with their start and end apart: 3 -> 2, of which waited for: 3 -> 2; matrix products, arithmetic and copies ran while one was open for 0% -> 0% of each run, Pallas kernels for 0% -> 0%
where the time goes in v1:
time: 413 us; the launch traced here: 412 us
  blocking collectives  306 us (74%)
  waiting for transfers between devices  37.1 us (9%)
  local copies, waits for them, and re-layouts  25.9 us (6%)
  starting transfers between devices  15.7 us (4%)
  between operations  13.5 us (3%)
  other arithmetic  10.1 us (2%)
    all_to_all x1, blocking collectives, shards(): lax.all_to_all(jnp.stack([symmetric] * lax.axis_size('pair')), 'pair', 0, 0)  203 us
    all_to_all x1, blocking collectives, shards(): lax.all_to_all(spread, 'pair', split_axis=0, concat_axis=2, tiled=True)  103 us
    reduce_scatter x1, waiting for transfers between devices, shards(): summed = lax.psum_scatter(routed, 'virt', scatter_dimension=1, tiled=True)  33.2 us
    ppermute x1, starting transfers between devices, from_partner(): return lax.ppermute(value, axis, pairs)  15.7 us
    all_to_all x3, local copies, waits for them, and re-layouts, shards(): lax.all_to_all(spread, 'pair', split_axis=0, concat_axis=2, tiled=True)  11.8 us
  transfers between devices with their start and end apart: 2, of which 2 were waited for; matrix products, arithmetic and copies ran while one was open for 0% of the time, Pallas kernels for 0%

profile of v1, /device:TPU:8, one launch (start us, length us, event | category | flops | bytes accessed | tf_op | source)
XLA Modules:
  0.0 412.3 jit_solution(597661854694317441)
XLA Ops:
  6.5 0.0 reduce-scatter.2.cloned.1.call-start
  6.5 15.7 %collective-permute-start = (bf16[8,1,4096]{2,0,1:T(8,128)(2,1)}, bf16[8,1,4096]{2,0,1:T(8,128)(2,1)S(1)}, u32[]{:S(2)}, u32[]{:S(2)}) collective-permute-start(bf16[8,1,4096]{2,0,1:T(8,128)(2,1)} %param.5), channel_id=1, source_target_pairs={{0,256},{8,264},{16,272},{24,280},{32,288},{40,296},{48,304},{56,3... | collective-permute-start | bytes 196616 | tf_op jit(solution)/shard_map/ppermute | solution.py:12
  22.3 0.7 compare_and_fusion
  22.9 3.8 collective-permute-done
  26.8 0.6 gather_fusion
  27.4 0.2 gather.7
  27.5 0.1 convert_bitcast_fusion
  27.6 0.1 copy.21
  27.8 0.1 reshape.44
  27.9 0.9 fusion.3
  28.8 0.5 stack.2
  29.3 0.0 copy-start.2
  29.3 202.8 %all_to_all.23 = bf16[64,8,1,4096]{3,1,2,0:T(8,128)(2,1)S(1)} all-to-all(bf16[64,8,1,4096]{3,1,2,0:T(8,128)(2,1)S(1)} %stack.2), channel_id=1, replica_groups=mesh['pair'=64,'virt'=8] {'pair'}, dimensions={0} | all-to-all | bytes 8388608 | tf_op jit(solution)/shard_map/all_to_all | solution.py:27
  232.1 0.0 copy-done.2
  232.1 0.0 copy-start
  232.1 0.0 copy-start.1
  232.1 2.8 fusion
  234.9 0.0 copy-done
  235.0 0.0 copy-done.1
  235.0 1.1 convolution_bitcast_fusion
  236.1 4.2 %copy.23 = f32[512,16,64]{2,1,0:T(8,128)} copy(f32[512,16,64]{0,1,2:T(8,128)S(1)} %convolution_bitcast_fusion) | data formatting | bytes 4194304 | tf_op jit(solution)/shard_map/pkj,ks->psj/transpose | solution.py:32
  240.2 4.6 %reshape.60 = f32[64,1,8192]{2,1,0:T(1,128)S(1)} reshape(f32[512,16,64]{2,1,0:T(8,128)} %copy.23) | data formatting | bytes 4194304
  244.8 103.2 %all_to_all.24 = f32[64,1,8192]{2,1,0:T(1,128)} all-to-all(f32[64,1,8192]{2,1,0:T(1,128)S(1)} %reshape.60), channel_id=1, replica_groups=mesh['pair'=64,'virt'=8] {'pair'}, dimensions={0} | all-to-all | bytes 4194304 | tf_op jit(solution)/shard_map/all_to_all | solution.py:33
  348.0 0.5 broadcast.48
  348.6 7.5 %reduce = f32[64,8192]{1,0:T(8,128)S(1)} reduce(f32[64,1,8192]{2,1,0:T(1,128)} %all_to_all.24, f32[]{:T(128)} %broadcast.48), dimensions={1}, to_apply=%all_to_all.17.reduce_sub_computation | reduce | bytes 4194308 | tf_op jit(solution)/shard_map/all_to_all | solution.py:33
  356.1 3.1 reshape.61
  359.2 6.5 %copy.27 = f32[8,16,64,64]{3,2,0,1:T(8,128)} copy(f32[8,16,64,64]{3,1,0,2:T(8,128)} %bitcast.27) | data formatting | bytes 4194304 | tf_op jit(solution)/shard_map/all_to_all | solution.py:33
  365.7 4.8 %reshape.59 = f32[8,16,4096]{2,0,1:T(8,128)} reshape(f32[8,16,64,64]{3,2,0,1:T(8,128)} %copy.27) | data formatting | bytes 4194304 | tf_op jit(solution)/shard_map/all_to_all | solution.py:33
  370.5 0.0 reduce-scatter.2.cloned.1.call-update
  370.5 33.2 %reduce-scatter.2.cloned.1.call-done = f32[8,2,4096]{2,0,1:T(8,128)} async-done(((f32[8,16,4096]{2,0,1:T(8,128)}), f32[8,2,4096]{2,0,1:T(8,128)}) %reduce-scatter.2.cloned.1.call-update) | async-done | bytes 262160 | tf_op jit(solution)/shard_map/reduce_scatter | solution.py:34
  403.7 1.0 convert_element_type.35
  404.7 0.8 copy.26
  (1 shorter events, 0.0 us)
Async XLA Ops:
  6.5 397.2 %reduce-scatter.2.cloned.1.call-start = ((), (), s32[]{:S(2)}) async-start(), calls=%async_computation.3 | async-start | bytes 2359296 | tf_op jit(solution)/shard_map/reduce_scatter | solution.py:34
  6.5 20.2 %collective-permute-start = (bf16[8,1,4096]{2,0,1:T(8,128)(2,1)}, bf16[8,1,4096]{2,0,1:T(8,128)(2,1)S(1)}, u32[]{:S(2)}, u32[]{:S(2)}) collective-permute-start(bf16[8,1,4096]{2,0,1:T(8,128)(2,1)} %param.5), channel_id=1, source_target_pairs={{0,256},{8,264},{16,272},{24,280},{32,288},{40,296},{48,304},{56,3... | collective-permute-start | bytes 196616 | tf_op jit(solution)/shard_map/ppermute | solution.py:12
  29.3 202.8 %copy-start.2 = (bf16[8,64,4096]{2,1,0:T(8,128)(2,1)S(1)}, bf16[8,64,4096]{2,1,0:T(8,128)(2,1)}, u32[]{:S(2)}) copy-start(bf16[8,64,4096]{2,1,0:T(8,128)(2,1)} %param.7) | copy-start | bytes 12582916
  232.1 2.9 copy-start
  232.1 2.9 copy-start.1
Sparse Core Ops, SparseCore 0:
  370.6 33.0 reduce-scatter.1
